TPU v7x, 32 devices: a whole 2x2x4 slice. The times are simulated.
32 devices in a mesh: groups: 2 (over y), psg: 16 (over z, x, core).
Axes of the slice: x: 2, y: 2, z: 4, core: 2. Of those that a mesh axis runs over, the one named last changes fastest.
Arguments:
- tail_hidden_states: bfloat16 [256, 8192], P('groups', 'psg'), parts along dimension 0, may hold values from -6 to 6
- passage_hidden_states: bfloat16 [2048, 8192], P(('groups', 'psg')), parts along dimension 0, may hold values from -6 to 6
- lengths: int32 [4], P('groups'), parts along dimension 0, may hold values from 1 to 768, 1024 in all
- storage_order: int32 [4], P('groups'), parts along dimension 0, may hold values from 0 to 1, each once
- orders: int32 [6, 2], P('groups'), parts along dimension 0, may hold values from 0 to 1, each once within a row
- w_query: bfloat16 [8192, 4096], P('psg'), may hold values from -1 to 1
- key_weight: bfloat16 [8192, 512], P('psg'), may hold values from -0.0625 to 0.0625
- value_weight: bfloat16 [8192, 512], P('psg'), may hold values from -0.0625 to 0.0625
- w_out: bfloat16 [4096, 8192], P(None, 'psg'), may hold values from -0.09375 to 0.09375
- norm_gain: float32 [8192], P('psg'), may hold values from 0.1 to 1.9
Outputs:
- layer_out: bfloat16 [256, 8192], P('groups', 'psg'), parts along dimension 0
There are 2 independent parts, one for each index of `groups`. A program takes and returns all parts, laid end to end along the dimension named above; an argument that names none is the same for every part. Nothing has to cross between parts.
Inputs may be any that keep to these rules, and one draw needn't show every extreme that they name: `lengths`: they sum to 1024; the largest is 768. `storage_order`: A permutation of the passages. `orders`: each row is a permutation of the passages.
All inputs are finite; a program needn't handle non-finite values.
Results may differ from a plain program's by a relative error of at most 0.01065.
The roundings to bfloat16 on the way count: a program that leaves them out, or rounds other values in their place, can miss the bound.
Values may be sent and summed in bfloat16 or wider, within the bound.
No kernel may reach another device: no remote copies, remote signals or barrier semaphores. Data moves between devices by JAX's collectives and lax.ppermute only.
A program may use at most 128 MiB of HBM per device.

v0:
```python
import jax
import jax.numpy as jnp
from jax import lax
from jax.sharding import PartitionSpec as P

MODEL_WIDTH = 8192
HEAD_SIZE = 128
theta_base = 500000.0
epsilon = 1e-05


def joined(part, axis, combine):
    gathered = jax.tree.map(lambda a: lax.all_gather(a, axis), part)

    def take(source):
        return jax.tree.map(lambda a: lax.dynamic_index_in_dim(a, source, 0, False), gathered)

    return lax.fori_loop(
        1, lax.axis_size(axis), lambda source, state: combine(state, take(source)), take(0)
    )


def rotate(vectors, places):
    half = vectors.shape[-1] // 2
    freqs = theta_base ** (-jnp.arange(half, dtype=jnp.float32) * 2.0 / vectors.shape[-1])
    angles = places.astype(jnp.float32)[:, None] * freqs[None, :]
    cosine = jnp.cos(angles)[:, None, :]
    sine = jnp.sin(angles)[:, None, :]
    first = vectors[..., :half]
    second = vectors[..., half:]
    return jnp.concatenate(
        [first * cosine - second * sine, second * cosine + first * sine], axis=-1
    )


def per_device(
    tail_hidden_states,
    passage_hidden_states,
    lengths,
    storage_order,
    orders,
    w_query,
    key_weight,
    value_weight,
    w_out,
    norm_gain,
):
    shards = lax.axis_size("psg")
    device = lax.axis_index("psg")
    row_count = passage_hidden_states.shape[0]
    tail_count = tail_hidden_states.shape[0]
    kv_heads = key_weight.shape[1] // HEAD_SIZE
    query_heads = w_query.shape[1] // HEAD_SIZE
    query_group = query_heads // kv_heads
    total_keys = row_count * shards
    query_part = jnp.dot(tail_hidden_states, w_query, preferred_element_type=jnp.float32)
    key_part = jnp.dot(tail_hidden_states, key_weight, preferred_element_type=jnp.float32)
    value_part = jnp.dot(tail_hidden_states, value_weight, preferred_element_type=jnp.float32)
    query_sum, key_sum, value_sum = lax.psum((query_part, key_part, value_part), "psg")
    tail_pos = total_keys + jnp.arange(tail_count, dtype=jnp.int32)
    query_vectors = rotate(query_sum.reshape(tail_count, query_heads, HEAD_SIZE), tail_pos).astype(
        jnp.bfloat16
    )
    query_vectors = query_vectors.reshape(tail_count, kv_heads, query_group, HEAD_SIZE)
    tail_key_rows = rotate(key_sum.reshape(tail_count, kv_heads, HEAD_SIZE), tail_pos).astype(
        jnp.bfloat16
    )
    tail_value_rows = value_sum.astype(jnp.bfloat16).reshape(tail_count, kv_heads, HEAD_SIZE)

    def add_block(piece):
        return jnp.dot(passage_hidden_states, piece, preferred_element_type=jnp.float32)

    unrotated_key = add_block(lax.all_gather(key_weight, "psg", axis=0, tiled=True))
    raw_value = add_block(lax.all_gather(value_weight, "psg", axis=0, tiled=True))
    numbers = jnp.arange(lengths.shape[0], dtype=jnp.int32)
    pick = (storage_order[:, None] == numbers[None, :]).astype(jnp.int32)
    stored_lengths = jnp.sum(pick * lengths[None, :], axis=1)
    ends = jnp.cumsum(stored_lengths)
    starts = ends - stored_lengths
    row_ids = device * row_count + jnp.arange(row_count, dtype=jnp.int32)
    slots = jnp.sum((ends[None, :] <= row_ids[:, None]).astype(jnp.int32), axis=1)
    in_slot = (slots[:, None] == numbers[None, :]).astype(jnp.int32)
    offsets = row_ids - jnp.sum(in_slot * starts[None, :], axis=1)
    passage_hot = jnp.dot(in_slot, pick)
    ordered_hot = (orders[:, :, None] == numbers[None, None, :]).astype(jnp.int32)
    ordered_lengths = jnp.sum(ordered_hot * lengths[None, None, :], axis=2)
    order_starts = jnp.cumsum(ordered_lengths, axis=1) - ordered_lengths
    placed = jnp.sum(ordered_hot * order_starts[:, :, None], axis=1)
    token_positions = (
        jnp.sum(passage_hot[None, :, :] * placed[:, None, :], axis=2) + offsets[None, :]
    )
    passage_values = raw_value.astype(jnp.bfloat16).reshape(row_count, kv_heads, HEAD_SIZE)
    unrotated_key = unrotated_key.reshape(row_count, kv_heads, HEAD_SIZE)
    scale = HEAD_SIZE ** (-0.5)
    tail_scores = (
        jnp.einsum(
            "tkgd,skd->tkgs", query_vectors, tail_key_rows, preferred_element_type=jnp.float32
        )
        * scale
    )
    causal = jnp.arange(tail_count)[None, :] <= jnp.arange(tail_count)[:, None]
    tail_scores = jnp.where(causal[:, None, None, :], tail_scores, -1e30)
    tail_top = jnp.max(tail_scores, axis=-1)

    def scores_for(places):
        keys = rotate(unrotated_key, places).astype(jnp.bfloat16)
        return (
            jnp.einsum("tkgd,nkd->tkgn", query_vectors, keys, preferred_element_type=jnp.float32)
            * scale
        )

    def local_stats(places):
        scores = scores_for(places)
        peak = jnp.maximum(jnp.max(scores, axis=-1), tail_top)
        return (peak, jnp.sum(jnp.exp(scores - peak[..., None]), axis=-1))

    def combine(first, second):
        peak = jnp.maximum(first[0], second[0])
        return (peak, first[1] * jnp.exp(first[0] - peak) + second[1] * jnp.exp(second[0] - peak))

    peaks, totals = joined(lax.map(local_stats, token_positions), "psg", combine)

    def accumulate(running, inputs):
        places, peak, partial_value = inputs
        weights = jnp.exp(scores_for(places) - peak[..., None])
        tail_weights = jnp.exp(tail_scores - peak[..., None])
        denom = (partial_value + jnp.sum(tail_weights, axis=-1))[..., None]
        shared = jnp.einsum(
            "tkgn,nkd->tkgd",
            weights.astype(jnp.bfloat16),
            passage_values,
            preferred_element_type=jnp.float32,
        )
        own = jnp.einsum(
            "tkgs,skd->tkgd",
            tail_weights.astype(jnp.bfloat16),
            tail_value_rows,
            preferred_element_type=jnp.float32,
        )
        return ((running[0] + shared / denom, running[1] + own / denom), None)

    start_sums = jnp.zeros((tail_count, kv_heads, query_group, HEAD_SIZE), jnp.float32)
    (shared_sum, own_sum), unused_slot = lax.scan(
        accumulate, (start_sums, start_sums), (token_positions, peaks, totals)
    )
    agreed_output = lax.psum(shared_sum, "psg") + own_sum
    mixed = agreed_output.reshape(tail_count, -1).astype(jnp.bfloat16)
    projected = jnp.dot(mixed, w_out, preferred_element_type=jnp.float32)
    squares = lax.psum(jnp.sum(projected * projected, axis=1), "psg")
    factor = lax.rsqrt(squares / MODEL_WIDTH + epsilon)[:, None]
    return (projected * factor * norm_gain[None, :]).astype(jnp.bfloat16)


def solution(mesh):
    placed = (
        P("groups", "psg"),
        P(("groups", "psg"), None),
        P("groups"),
        P("groups"),
        P("groups", None),
        P("psg", None),
        P("psg", None),
        P("psg", None),
        P(None, "psg"),
        P("psg"),
    )
    return jax.shard_map(
        per_device, mesh=mesh, in_specs=placed, out_specs=P("groups", "psg"), check_vma=False
    )
```

profile of v0, /device:TPU:0, one launch (start us, length us, event | category | flops | bytes accessed | tf_op | source)
XLA Modules:
  0.0 503.8 jit_solution(18444703325682669474)
XLA Ops:
  6.5 1.4 convolution_bitcast_fusion.1
  8.7 3.0 convolution_bitcast_fusion
  11.7 1.7 copy.65
  16.5 66.6 %all-reduce.8 = bf16[128,512]{1,0:T(8,128)(2,1)S(1)} all-reduce(f32[128,512]{1,0:T(8,128)S(1)} %fusion.42), channel_id=1, replica_groups=mesh['groups'=2,'psg'=16] {'psg'}, use_global_device_ids=true, to_apply=%region_17.18 | all-reduce | flops 65536 | bytes 393216 | tf_op jit(solution)/shard_map/psum | solution.py:59
  84.0 32.4 %all-reduce.7.cloned.1.call-done = (f32[128,32,128]{2,1,0:T(8,128)}, f32[128,4,128]{2,0,1:T(8,128)}) async-done(((f32[128,32,128]{2,1,0:T(8,128)}, f32[128,4,128]{2,0,1:T(8,128)}), (f32[128,32,128]{2,1,0:T(8,128)}, f32[128,4,128]{2,0,1:T(8,128)})) %all-reduce.7.cloned.1.call-update) | async-done | bytes 2359312 | tf_op jit(solution)/shard_map/psum | solution.py:59
  116.5 3.0 subtract_convert_fusion.2
  121.4 1.8 fusion.41
  123.3 1.9 copy.52
  125.2 66.9 %all-gather.5.cloned.1.call-done = bf16[8192,512]{1,0:T(8,128)(2,1)} async-done(((bf16[512,512]{1,0:T(8,128)(2,1)}), bf16[8192,512]{1,0:T(8,128)(2,1)}) %all-gather.5.cloned.1.call-update) | async-done | bytes 8388624 | tf_op jit(solution)/shard_map/all_gather | solution.py:73
  192.1 4.9 convolution_bitcast_fusion.2
  197.1 70.1 %all-gather.7.cloned.1.call-done = bf16[8192,512]{1,0:T(8,128)(2,1)} async-done(((bf16[512,512]{1,0:T(8,128)(2,1)}), bf16[8192,512]{1,0:T(8,128)(2,1)}) %all-gather.7.cloned.1.call-update) | async-done | bytes 8388624 | tf_op jit(solution)/shard_map/all_gather | solution.py:74
  267.2 4.9 fusion.31
  272.8 7.1 %while.46 = (s32[]{:T(128)}, f32[3,128,4,8]{1,3,2,0:T(8,128)S(1)}, f32[3,128,4,8]{1,3,2,0:T(8,128)S(1)}, f32[64,4,128]{2,0,1:T(8,128)S(1)}, s32[3,64]{1,0:T(4,12...) while((s32[]{:T(128)}, f32[3,128,4,8]{1,3,2,0:T(8,128)S(1)}, ...), condition=%wide.region_14.15_spmd, body=%wide.region_11.14_spmd.sunk | while | flops 68419776 | bytes 3622249 | solution.py:121
  273.1 1.8 fusion.73
  275.5 1.8 fusion.73
  277.8 1.8 fusion.73
  279.9 21.2 %all-gather.1 = f32[48,128,4,8]{1,3,2,0:T(8,128)S(1)} all-gather(f32[3,128,4,8]{1,3,2,0:T(8,128)S(1)} %get-tuple-element.367), channel_id=3, replica_groups=mesh['groups'=2,'psg'=16] {'psg'}, dimensions={0}, use_global_device_ids=true | all-gather | bytes 835584 | tf_op jit(solution)/shard_map/all_gather | solution.py:13
  301.0 20.4 %all-gather = f32[48,128,4,8]{1,3,2,0:T(8,128)S(1)} all-gather(f32[3,128,4,8]{1,3,2,0:T(8,128)S(1)} %get-tuple-element.366), channel_id=2, replica_groups=mesh['groups'=2,'psg'=16] {'psg'}, dimensions={0}, use_global_device_ids=true | all-gather | bytes 835584 | tf_op jit(solution)/shard_map/all_gather | solution.py:13
  322.3 13.5 %while.47 = (s32[]{:T(128)}, f32[3,128,4,8]{1,3,2,0:T(8,128)S(1)}, f32[3,128,4,8]{1,3,2,0:T(8,128)S(1)}, f32[16,3,128,4,8]{2,4,3,1,0:T(8,128)}, f32[16,3,128,4,8...) while((s32[]{:T(128)}, f32[3,128,4,8]{1,3,2,0:T(8,128)S(1)}, f32[3,128,4,8]{1,3,2,0:T(8,128)S(1)}, ...), condition=%wide.region_16.17_spmd, body=%wide.region_15.16_spmd.sunk | while | flops 73733 | bytes 295035 | solution.py:18
  335.8 27.7 %while.48 = (s32[]{:T(128)}, f32[128,4,8,128]{3,0,2,1:T(8,128)}, f32[128,4,8,128]{3,0,2,1:T(8,128)}, f32[64,4,128]{2,0,1:T(8,128)S(1)}, s32[3,64]{1,0:T(4,128)S(...) while((s32[]{:T(128)}, f32[128,4,8,128]{3,0,2,1:T(8,128)}, ...), condition=%wide.region_20.21_spmd.clone, body=%wide.region_18.20_spmd.clone.sunk | while | flops 274731200 | bytes 14337436 | solution.py:143
  335.9 1.3 fusion.79
  337.5 3.7 fusion.81
  341.2 3.2 fusion.82
  346.0 4.4 fusion.81
  350.4 3.5 fusion.82
  355.6 4.4 fusion.81
  360.0 3.5 fusion.82
  363.5 2.9 copy.54
  366.5 1.9 copy.55
  368.4 94.1 %all-reduce.5.cloned.1.call-done = f32[128,4,8,128]{0,3,2,1:T(8,128)} async-done(((f32[128,4,8,128]{0,3,2,1:T(8,128)}), f32[128,4,8,128]{0,3,2,1:T(8,128)}) %all-reduce.5.cloned.1.call-update) | async-done | bytes 2097168 | tf_op jit(solution)/shard_map/psum | solution.py:146
  462.5 2.0 add_convert_fusion.2
  466.2 30.4 %psum.39 = f32[128]{0:T(128)S(1)} all-reduce(f32[128]{0:T(128)S(1)} %get-tuple-element.550), channel_id=1, replica_groups=mesh['groups'=2,'psg'=16] {'psg'}, use_global_device_ids=true, to_apply=%region_23.24 | all-reduce | flops 128 | bytes 1024 | tf_op jit(solution)/shard_map/psum | solution.py:149
  (125 shorter events, 28.8 us)
Async XLA Ops:
  6.5 185.6 %copy-start = (bf16[64,8192]{1,0:T(8,128)(2,1)S(1)}, bf16[64,8192]{1,0:T(8,128)(2,1)}, u32[]{:S(2)}) copy-start(bf16[64,8192]{1,0:T(8,128)(2,1)} %param.17) | copy-start | bytes 3145732
  6.5 109.9 %all-reduce.7.cloned.1.call-start = ((), (), s32[]{:S(2)}) async-start(), calls=%async_computation.3 | async-start | bytes 4718592 | tf_op jit(solution)/shard_map/psum | solution.py:59
  13.4 1.6 copy-start.10
  13.4 1.6 copy-start.11
  13.4 2.0 copy-start.8
  13.4 2.2 copy-start.3
  13.4 2.2 copy-start.6
  13.4 178.7 %all-gather.5.cloned.1.call-start = ((), (), s32[]{:S(2)}) async-start(), calls=%async_computation | async-start | bytes 8912896 | tf_op jit(solution)/shard_map/all_gather | solution.py:73
  14.2 253.0 %all-gather.7.cloned.1.call-start = ((), (), s32[]{:S(2)}) async-start(), calls=%async_computation.1 | async-start | bytes 8912896 | tf_op jit(solution)/shard_map/all_gather | solution.py:74
  14.9 447.6 %all-reduce.5.cloned.1.call-start = ((), (), s32[]{:S(2)}) async-start(), calls=%async_computation.2 | async-start | bytes 4194304 | tf_op jit(solution)/shard_map/psum | solution.py:146
  120.3 1.0 copy-start.7
  120.9 2.3 copy-start.1
  301.0 20.4 %copy-start.4 = (f32[48,128,4,8]{1,3,2,0:T(8,128)}, f32[48,128,4,8]{1,3,2,0:T(8,128)S(1)}, u32[]{:S(2)}) copy-start(f32[48,128,4,8]{1,3,2,0:T(8,128)S(1)} %all-gather.1) | copy-start | bytes 2359300
  321.5 0.9 copy-start.5
  462.5 2.8 copy-start.2
  465.3 31.2 %copy-start.9 = (f32[512]{0:T(512)S(1)}, f32[512]{0:T(512)}, u32[]{:S(2)}) copy-start(f32[512]{0:T(512)} %param.25) | copy-start | bytes 6148
Sparse Core Ops, SparseCore 0:
  13.6 102.8 all-reduce.6
  118.6 73.4 all-gather.4
  194.3 72.8 all-gather.6
  366.6 95.8 all-reduce.4
where the time goes:
time: 505 us; the launch traced here: 504 us
  waiting for transfers between devices  265 us (52%)
  blocking collectives  139 us (28%)
  matrix products  45.4 us (9%)
  other arithmetic  27.3 us (5%)
  local copies, waits for them, and re-layouts  13.5 us (3%)
  between operations  13.4 us (3%)
    psum x1, waiting for transfers between devices, per_device(): agreed_output = lax.psum(shared_sum, 'psg') + own_sum  94.1 us
    all_gather x1, waiting for transfers between devices, per_device(): lax.all_gather(value_weight, 'psg', axis=0, tiled=True)  70.1 us
    all_gather x1, waiting for transfers between devices, per_device(): lax.all_gather(key_weight, 'psg', axis=0, tiled=True)  66.9 us
    psum x1, blocking collectives, per_device(): lax.psum((query_part, key_part, value_part), 'psg')  66.6 us
    all_gather x2, blocking collectives, joined(): gathered = jax.tree.map(lambda a: lax.all_gather(a, axis), part)  41.6 us
    psum x1, waiting for transfers between devices, per_device(): lax.psum((query_part, key_part, value_part), 'psg')  32.4 us
    psum x1, blocking collectives, per_device(): squares = lax.psum(jnp.sum(projected * projected, axis=1), 'psg')  30.4 us
    add x15, other arithmetic, combine(): first[1] * jnp.exp(first[0] - peak) + second[1] * jnp.exp(second[0] - peak)  13.2 us
  transfers between devices with their start and end apart: 4, of which 4 were waited for; matrix products, arithmetic and copies ran while one was open for 3% of the time, Pallas kernels for 0%

commit v1 on v0

--- a/solution.py
+++ b/solution.py
@@ -143,7 +143,7 @@
     (shared_sum, own_sum), unused_slot = lax.scan(
         accumulate, (start_sums, start_sums), (token_positions, peaks, totals)
     )
-    agreed_output = lax.psum(shared_sum, "psg") + own_sum
+    agreed_output = jnp.sum(lax.all_gather(shared_sum, "psg"), axis=0) + own_sum
     mixed = agreed_output.reshape(tail_count, -1).astype(jnp.bfloat16)
     projected = jnp.dot(mixed, w_out, preferred_element_type=jnp.float32)
     squares = lax.psum(jnp.sum(projected * projected, axis=1), "psg")

time: 505 us -> 588 us (1.16)
  waiting for transfers between devices: 265 us -> 337 us
  other arithmetic: 27.3 us -> 39 us
    all_gather x0 -> x1, waiting for transfers between devices: none -> 166 us  [per_device(): agreed_output = jnp.sum(lax.all_gather(shared_sum, 'psg'), axis=0) + own_sum]
    psum x1 -> x0, waiting for transfers between devices: 94.1 us -> none  [per_device(): agreed_output = lax.psum(shared_sum, 'psg') + own_sum]
    reduce_sum x0 -> x1, other arithmetic: none -> 11.8 us  [per_device(): agreed_output = jnp.sum(lax.all_gather(shared_sum, 'psg'), axis=0) + own_sum]
where the time goes in v1:
time: 588 us; the launch traced here: 586 us
  waiting for transfers between devices  337 us (57%)
  blocking collectives  140 us (24%)
  matrix products  46.6 us (8%)
  other arithmetic  39 us (7%)
  between operations  13.4 us (2%)
  local copies, waits for them, and re-layouts  8.51 us (1%)
    all_gather x1, waiting for transfers between devices, per_device(): agreed_output = jnp.sum(lax.all_gather(shared_sum, 'psg'), axis=0) + own_sum  166 us
    all_gather x1, waiting for transfers between devices, per_device(): lax.all_gather(value_weight, 'psg', axis=0, tiled=True)  70.1 us
    all_gather x1, waiting for transfers between devices, per_device(): lax.all_gather(key_weight, 'psg', axis=0, tiled=True)  66.9 us
    psum x1, blocking collectives, per_device(): lax.psum((query_part, key_part, value_part), 'psg')  66.5 us
    all_gather x2, blocking collectives, joined(): gathered = jax.tree.map(lambda a: lax.all_gather(a, axis), part)  41.2 us
    psum x1, blocking collectives, per_device(): squares = lax.psum(jnp.sum(projected * projected, axis=1), 'psg')  32.6 us
    psum x1, waiting for transfers between devices, per_device(): lax.psum((query_part, key_part, value_part), 'psg')  32.4 us
    add x15, other arithmetic, combine(): first[1] * jnp.exp(first[0] - peak) + second[1] * jnp.exp(second[0] - peak)  13.2 us
  transfers between devices with their start and end apart: 4, of which 4 were waited for; matrix products, arithmetic and copies ran while one was open for 3% of the time, Pallas kernels for 0%

profile of v1, /device:TPU:0, one launch (start us, length us, event | category | flops | bytes accessed | tf_op | source)
XLA Modules:
  0.0 586.0 jit_solution(15592702222840255161)
XLA Ops:
  6.5 1.4 convolution_bitcast_fusion.1
  8.7 3.0 convolution_bitcast_fusion
  11.7 1.7 copy.62
  16.4 66.5 %all-reduce.5 = bf16[128,512]{1,0:T(8,128)(2,1)S(1)} all-reduce(f32[128,512]{1,0:T(8,128)S(1)} %fusion.42), channel_id=1, replica_groups=mesh['groups'=2,'psg'=16] {'psg'}, use_global_device_ids=true, to_apply=%region_17.18 | all-reduce | flops 65536 | bytes 393216 | tf_op jit(solution)/shard_map/psum | solution.py:59
  84.0 32.4 %all-reduce.4.cloned.1.call-done = (f32[128,32,128]{2,1,0:T(8,128)}, f32[128,4,128]{2,0,1:T(8,128)}) async-done(((f32[128,32,128]{2,1,0:T(8,128)}, f32[128,4,128]{2,0,1:T(8,128)}), (f32[128,32,128]{2,1,0:T(8,128)}, f32[128,4,128]{2,0,1:T(8,128)})) %all-reduce.4.cloned.1.call-update) | async-done | bytes 2359312 | tf_op jit(solution)/shard_map/psum | solution.py:59
  116.4 3.0 subtract_convert_fusion.2
  121.4 1.8 fusion.41
  123.2 1.9 copy.50
  125.2 66.9 %all-gather.7.cloned.1.call-done = bf16[8192,512]{1,0:T(8,128)(2,1)} async-done(((bf16[512,512]{1,0:T(8,128)(2,1)}), bf16[8192,512]{1,0:T(8,128)(2,1)}) %all-gather.7.cloned.1.call-update) | async-done | bytes 8388624 | tf_op jit(solution)/shard_map/all_gather | solution.py:73
  192.1 4.9 convolution_bitcast_fusion.2
  197.0 70.1 %all-gather.9.cloned.1.call-done = bf16[8192,512]{1,0:T(8,128)(2,1)} async-done(((bf16[512,512]{1,0:T(8,128)(2,1)}), bf16[8192,512]{1,0:T(8,128)(2,1)}) %all-gather.9.cloned.1.call-update) | async-done | bytes 8388624 | tf_op jit(solution)/shard_map/all_gather | solution.py:74
  267.1 4.9 fusion.31
  272.7 7.1 %while.46 = (s32[]{:T(128)}, f32[3,128,4,8]{1,3,2,0:T(8,128)S(1)}, f32[3,128,4,8]{1,3,2,0:T(8,128)S(1)}, f32[64,4,128]{2,0,1:T(8,128)S(1)}, s32[3,64]{1,0:T(4,12...) while((s32[]{:T(128)}, f32[3,128,4,8]{1,3,2,0:T(8,128)S(1)}, ...), condition=%wide.region_14.15_spmd, body=%wide.region_11.14_spmd.sunk | while | flops 68419776 | bytes 3622249 | solution.py:121
  273.0 1.8 fusion.73
  275.4 1.8 fusion.73
  277.8 1.8 fusion.73
  279.8 21.3 %all-gather.1 = f32[48,128,4,8]{1,3,2,0:T(8,128)S(1)} all-gather(f32[3,128,4,8]{1,3,2,0:T(8,128)S(1)} %get-tuple-element.367), channel_id=3, replica_groups=mesh['groups'=2,'psg'=16] {'psg'}, dimensions={0}, use_global_device_ids=true | all-gather | bytes 835584 | tf_op jit(solution)/shard_map/all_gather | solution.py:13
  301.1 19.9 %all-gather = f32[48,128,4,8]{1,3,2,0:T(8,128)S(1)} all-gather(f32[3,128,4,8]{1,3,2,0:T(8,128)S(1)} %get-tuple-element.366), channel_id=2, replica_groups=mesh['groups'=2,'psg'=16] {'psg'}, dimensions={0}, use_global_device_ids=true | all-gather | bytes 835584 | tf_op jit(solution)/shard_map/all_gather | solution.py:13
  321.9 13.5 %while.47 = (s32[]{:T(128)}, f32[3,128,4,8]{1,3,2,0:T(8,128)S(1)}, f32[3,128,4,8]{1,3,2,0:T(8,128)S(1)}, f32[16,3,128,4,8]{2,4,3,1,0:T(8,128)}, f32[16,3,128,4,8...) while((s32[]{:T(128)}, f32[3,128,4,8]{1,3,2,0:T(8,128)S(1)}, f32[3,128,4,8]{1,3,2,0:T(8,128)S(1)}, ...), condition=%wide.region_16.17_spmd, body=%wide.region_15.16_spmd.sunk | while | flops 73733 | bytes 295035 | solution.py:18
  335.4 26.6 %while.48 = (s32[]{:T(128)}, f32[128,4,8,128]{3,0,2,1:T(8,128)}, f32[128,4,8,128]{3,0,2,1:T(8,128)}, f32[64,4,128]{2,0,1:T(8,128)S(1)}, s32[3,64]{1,0:T(4,128)S(...) while((s32[]{:T(128)}, f32[128,4,8,128]{3,0,2,1:T(8,128)}, ...), condition=%wide.region_20.21_spmd.clone, body=%wide.region_18.20_spmd.clone.sunk | while | flops 274731200 | bytes 14337436 | solution.py:143
  335.5 1.3 fusion.79
  337.1 3.2 fusion.81
  340.3 3.2 fusion.82
  345.2 4.0 fusion.81
  349.3 3.5 fusion.82
  354.4 4.0 fusion.81
  358.5 3.5 fusion.82
  362.0 166.5 %all-gather.11.cloned.1.call-done = f32[2048,4,8,128]{3,0,2,1:T(8,128)} async-done(((f32[128,4,8,128]{3,0,2,1:T(8,128)}), f32[2048,4,8,128]{3,0,2,1:T(8,128)}) %all-gather.11.cloned.1.call-update) | async-done | bytes 33554448 | tf_op jit(solution)/shard_map/all_gather | solution.py:146
  528.5 11.8 %reduce_sum.102 = f32[128,4,8,128]{3,0,2,1:T(8,128)S(1)} reduce(f32[16,128,4,8,128]{4,1,0,3,2:T(8,128)} %bitcast.158, f32[]{:T(128)} %constant.166.clone.1), dimensions={0}, to_apply=%region_21.22 | reduce | flops 7864320 | bytes 35651588 | tf_op jit(solution)/shard_map/reduce_sum | solution.py:146
  540.3 1.9 add_convert_fusion.2
  542.9 3.1 multiply_reduce_fusion
  546.0 32.6 %psum.31 = f32[128]{0:T(128)S(1)} all-reduce(f32[128]{0:T(128)S(1)} %get-tuple-element.550), channel_id=1, replica_groups=mesh['groups'=2,'psg'=16] {'psg'}, use_global_device_ids=true, to_apply=%region_23.24 | all-reduce | flops 128 | bytes 1024 | tf_op jit(solution)/shard_map/psum | solution.py:149
  (127 shorter events, 27.9 us)
Async XLA Ops:
  6.5 185.5 %copy-start = (bf16[64,8192]{1,0:T(8,128)(2,1)S(1)}, bf16[64,8192]{1,0:T(8,128)(2,1)}, u32[]{:S(2)}) copy-start(bf16[64,8192]{1,0:T(8,128)(2,1)} %param.17) | copy-start | bytes 3145732
  6.5 109.9 %all-reduce.4.cloned.1.call-start = ((), (), s32[]{:S(2)}) async-start(), calls=%async_computation.3 | async-start | bytes 4718592 | tf_op jit(solution)/shard_map/psum | solution.py:59
  13.3 1.6 copy-start.11
  13.3 1.6 copy-start.12
  13.3 2.0 copy-start.9
  13.3 2.2 copy-start.4
  13.3 2.2 copy-start.7
  13.4 178.7 %all-gather.7.cloned.1.call-start = ((), (), s32[]{:S(2)}) async-start(), calls=%async_computation | async-start | bytes 8912896 | tf_op jit(solution)/shard_map/all_gather | solution.py:73
  14.1 253.0 %all-gather.9.cloned.1.call-start = ((), (), s32[]{:S(2)}) async-start(), calls=%async_computation.1 | async-start | bytes 8912896 | tf_op jit(solution)/shard_map/all_gather | solution.py:74
  14.9 513.6 %all-gather.11.cloned.1.call-start = ((), (), s32[]{:S(2)}) async-start(), calls=%async_computation.2 | async-start | bytes 35651584 | tf_op jit(solution)/shard_map/all_gather | solution.py:146
  120.3 1.0 copy-start.8
  120.9 2.3 copy-start.2
  279.8 55.6 %copy-start.3 = (bf16[128,4,8,128]{3,0,2,1:T(8,128)(2,1)S(1)}, bf16[128,4,8,128]{3,0,2,1:T(8,128)(2,1)}, u32[]{:S(2)}) copy-start(bf16[128,4,8,128]{3,0,2,1:T(8,128)(2,1)} %get-tuple-element.816) | copy-start | bytes 3145732
  301.1 20.0 %copy-start.5 = (f32[48,128,4,8]{1,3,2,0:T(8,128)}, f32[48,128,4,8]{1,3,2,0:T(8,128)S(1)}, u32[]{:S(2)}) copy-start(f32[48,128,4,8]{1,3,2,0:T(8,128)S(1)} %all-gather.1) | copy-start | bytes 2359300
  321.0 0.9 copy-start.6
  542.9 36.5 %copy-start.1 = (bf16[64,8192]{1,0:T(8,128)(2,1)S(1)}, bf16[64,8192]{1,0:T(8,128)(2,1)}, u32[]{:S(2)}) copy-start(bf16[64,8192]{1,0:T(8,128)(2,1)} %param.17) | copy-start | bytes 3145732
  542.9 35.8 %copy-start.10 = (f32[512]{0:T(512)S(1)}, f32[512]{0:T(512)}, u32[]{:S(2)}) copy-start(f32[512]{0:T(512)} %param.25) | copy-start | bytes 6148
Sparse Core Ops, SparseCore 0:
  13.5 102.8 all-reduce.3
  118.6 73.4 all-gather.6
  194.2 72.8 all-gather.8
  362.1 166.3 all-gather.10
